TPU v7x, 512 devices: a whole 4x8x8 slice. The times are simulated.
512 devices in a mesh: segment: 32 (over y_lo, z), dp: 8 (over x, core), seq: 2 (over y_hi).
Axes of the slice: x: 4, y: 8 (y_hi: 2, y_lo: 4; y = y_hi * 4 + y_lo), z: 8, core: 2. Of those that a mesh axis runs over, the one named last changes fastest.
Arguments:
- stored_part_activation: bfloat16 [32, 2, 8, 256, 2048], P('segment', None, 'dp', 'seq'), may hold values from -64 to 64
- pending_sensitivity: bfloat16 [32, 8, 256, 2048], P('segment', 'dp', 'seq'), may hold values from -0.119628906 to 0.119628906
- uppermost_result_derivative: bfloat16 [1, 8, 256, 2048], P(None, 'dp', 'seq'), may hold values from -0.119628906 to 0.119628906
- scaling_factors: float32 [32, 4, 2048], P('segment'), may hold values from -0.5 to 5
- attended_tile_table: int32 [32, 2, 8, 2, 2], P('segment', None, 'dp'), may hold values from 0 to 1, as said below
- active_tile_number: int32 [32, 2, 8, 2], P('segment', None, 'dp'), may hold values from 1 to 2
Outputs:
- factor_derivatives: float32 [32, 4, 2048], P('segment')
Inputs may be any that keep to these rules, and one draw needn't show every extreme that they name: `attended_tile_table`: each list names every key block of its sample once; the allowed ones come first.
All inputs are finite; a program needn't handle non-finite values.
Results may differ from a plain program's by a relative error of at most 0.009.
Values may be sent and summed in bfloat16 or wider, within the bound.
A program may use at most 64 MiB of HBM per device.

v0:
```python
import jax
import jax.numpy as jnp
from jax import lax
from jax.sharding import PartitionSpec as P

HEAD_DIM = 128
BLK = 128
epsilon = 1e-06


def partner(block, axis, apart):
    count = lax.axis_size(axis)
    route = []
    for low in range(count):
        high = low | 1 << apart
        if high != low and high < count:
            route += [(low, high), (high, low)]
    return lax.ppermute(block, axis, route)


def from_behind(block, axis, distance):
    devices = range(lax.axis_size(axis))
    route = [(i - distance, i) for i in devices if i - distance in devices]
    return lax.ppermute(block, axis, route)


def normed_of(inputs):
    widened = inputs.astype(jnp.float32).reshape(
        inputs.shape[:-1] + (inputs.shape[-1] // HEAD_DIM, HEAD_DIM)
    )
    inv_rms = lax.rsqrt(jnp.mean(widened * widened, axis=-1, keepdims=True) + epsilon)
    return (widened * inv_rms, inv_rms)


def norm_back(grad_norm, norm_val, inv_rms):
    return inv_rms * (grad_norm - norm_val * jnp.mean(grad_norm * norm_val, axis=-1, keepdims=True))


def allowed_blocks(block_list, live_count):
    block_total = block_list.shape[0]
    live_slots = jnp.arange(block_total)[None, :] < live_count[:, None]
    matches = (block_list[:, :, None] == jnp.arange(block_total)[None, None, :]) & live_slots[
        :, :, None
    ]
    return jnp.any(matches, axis=1)


def token_mask(permitted, query_half, seq_index, dev_blocks):
    local_blocks = jnp.arange(dev_blocks, dtype=jnp.int32)
    query_rows = query_half * dev_blocks + local_blocks
    key_order = jnp.concatenate(
        [seq_index * dev_blocks + local_blocks, (1 - seq_index) * dev_blocks + local_blocks]
    )
    picked = permitted[query_rows[:, None], key_order[None, :]]
    return jnp.repeat(jnp.repeat(picked, BLK, axis=0), BLK, axis=1)


def attend(query_norm, key_norm, gain_heads, allowed, incoming, scaling):
    queries = (query_norm * gain_heads[0]).astype(jnp.bfloat16)
    key_mat = (key_norm * gain_heads[1]).astype(jnp.bfloat16)
    val_mat = (key_norm * gain_heads[2]).astype(jnp.bfloat16)
    scores = (
        jnp.einsum("thd,shd->hts", queries, key_mat, preferred_element_type=jnp.float32) * scaling
    )
    scores = jnp.where(allowed[None], scores, -jnp.inf)
    exped = jnp.exp(scores - jnp.max(scores, axis=-1, keepdims=True))
    probs = exped / jnp.sum(exped, axis=-1, keepdims=True)
    probs_low = probs.astype(jnp.bfloat16)
    output = jnp.einsum("hts,shd->thd", probs_low, val_mat, preferred_element_type=jnp.float32)
    grad_out = (gain_heads[3] * incoming).astype(jnp.bfloat16)
    grad_probs = jnp.einsum("thd,shd->hts", grad_out, val_mat, preferred_element_type=jnp.float32)
    grad_scores = (
        probs * (grad_probs - jnp.sum(probs * grad_probs, axis=-1, keepdims=True))
    ).astype(jnp.bfloat16)
    return (queries, key_mat, probs_low, output, grad_out, grad_scores)


def shards(
    stored_part_activation,
    pending_sensitivity,
    uppermost_result_derivative,
    scaling_factors,
    attended_tile_table,
    active_tile_number,
):
    segments = lax.axis_size("segment")
    segment_index = lax.axis_index("segment")
    seq_index = lax.axis_index("seq")
    window = stored_part_activation.shape[1]
    row_count = stored_part_activation.shape[3]
    channels = stored_part_activation.shape[4]
    head_count = channels // HEAD_DIM
    dev_blocks = row_count // BLK
    scaling = HEAD_DIM ** (-0.5)
    own_window = stored_part_activation[0, :, 0]
    gain_heads = scaling_factors[0].reshape(4, head_count, HEAD_DIM)
    incoming_sensitivity = pending_sensitivity[0, 0].astype(jnp.float32)
    totals = jnp.zeros((4, head_count, HEAD_DIM), jnp.float32)
    for step_index in range(window):
        own_rows = own_window[step_index]
        other_rows = partner(own_rows, "seq", 0)
        permitted = allowed_blocks(
            attended_tile_table[0, step_index, 0], active_tile_number[0, step_index, 0]
        )
        own_norm, own_inv = normed_of(own_rows)
        other_norm, other_inv = normed_of(other_rows)
        key_norm = jnp.concatenate([own_norm, other_norm], axis=0)
        incoming = incoming_sensitivity.reshape(row_count, head_count, HEAD_DIM)
        own_allowed = token_mask(permitted, seq_index, seq_index, dev_blocks)
        queries, key_mat, probs_low, output, grad_out, grad_scores = attend(
            own_norm, key_norm, gain_heads, own_allowed, incoming, scaling
        )
        grad_query = (
            jnp.einsum("hts,shd->thd", grad_scores, key_mat, preferred_element_type=jnp.float32)
            * scaling
        )
        grad_key = (
            jnp.einsum("hts,thd->shd", grad_scores, queries, preferred_element_type=jnp.float32)
            * scaling
        )
        grad_value = jnp.einsum(
            "hts,thd->shd", probs_low, grad_out, preferred_element_type=jnp.float32
        )
        key_part = grad_key * gain_heads[1] + grad_value * gain_heads[2]
        self_part = key_part[:row_count]
        key_terms = jnp.sum(grad_key * key_norm, axis=0)
        value_terms = jnp.sum(grad_value * key_norm, axis=0)
        if step_index < window - 1:
            lent = norm_back(key_part[row_count:], other_norm, other_inv).astype(jnp.bfloat16)
            returned = partner(lent, "seq", 0).astype(jnp.float32)
        grad_terms = jnp.stack(
            [
                jnp.sum(grad_query * own_norm, axis=0),
                key_terms,
                value_terms,
                jnp.sum(output * incoming, axis=0),
            ]
        )
        totals = totals + grad_terms
        if step_index < window - 1:
            grad_input = (
                incoming
                + norm_back(grad_query * gain_heads[0] + self_part, own_norm, own_inv)
                + returned
            )
            received = from_behind(grad_input.reshape(row_count, channels), "segment", -1)
            incoming_sensitivity = jnp.where(
                segment_index == segments - 1,
                uppermost_result_derivative[step_index, 0].astype(jnp.float32),
                received,
            )
    summed = lax.psum(totals.reshape(4, channels), ("dp", "seq"))
    return summed[None]


def solution(mesh):
    placed = (
        P("segment", None, "dp", "seq", None),
        P("segment", "dp", "seq", None),
        P(None, "dp", "seq", None),
        P("segment", None, None),
        P("segment", None, "dp", None, None),
        P("segment", None, "dp", None),
    )
    return jax.shard_map(
        shards, mesh=mesh, in_specs=placed, out_specs=P("segment", None, None), check_vma=False
    )
```

profile of v0, /device:TPU:24, one launch (start us, length us, event | category | flops | bytes accessed | tf_op | source)
XLA Modules:
  0.0 220.2 jit_solution(2187491883206557950)
XLA Ops:
  0.0 2.7 %slice_convert_fusion = (f32[1,1,1,128,2048]{4,3,2,1,0:T(8,128)}, bf16[128,2048]{1,0:T(8,128)(2,1)}, bf16[128,2048]{1,0:T(8,128)(2,1)}, f32[1,1,1,128,2048]{4,3,2,1,0:T(8,128)S(1)}) fusion(bf16[1,2,1,128,2048]{4,3,2,1,0:T(8,128)(2,1)} %param.6), kind=kLoop, calls=%fused_computation.75 | loop fusion | flops 524288 | bytes 4194304 | tf_op jit(solution)/shard_map/convert_element_type | solution.py:28
  2.7 5.0 %collective-permute-start = (bf16[128,2048]{1,0:T(8,128)(2,1)}, bf16[128,2048]{1,0:T(8,128)(2,1)}, u32[]{:S(2)}, u32[]{:S(2)}) collective-permute-start(bf16[128,2048]{1,0:T(8,128)(2,1)} %get-tuple-element.12), channel_id=1, source_target_pairs={{0,1},{1,0},{2,3},{3,2},{4,5},{5,4},{6,7},{7,6},{8,9},{9,8},{10,11... | collective-permute-start | bytes 1572872 | tf_op jit(solution)/shard_map/ppermute | solution.py:18
  7.8 4.7 %collective-permute-start.1 = (bf16[128,2048]{1,0:T(8,128)(2,1)}, bf16[128,2048]{1,0:T(8,128)(2,1)}, u32[]{:S(2)}, u32[]{:S(2)}) collective-permute-start(bf16[128,2048]{1,0:T(8,128)(2,1)} %get-tuple-element.13), channel_id=1, source_target_pairs={{0,1},{1,0},{2,3},{3,2},{4,5},{5,4},{6,7},{7,6},{8,9},{9,8},{10,11... | collective-permute-start | bytes 1572872 | tf_op jit(solution)/shard_map/ppermute | solution.py:18
  12.5 0.1 pad_bitcast_fusion
  12.6 0.2 or_reduce_fusion
  12.8 0.0 copy-done.13
  12.8 0.0 copy-done.12
  12.8 0.1 iota_compare_fusion
  12.9 0.1 and_reduce_fusion.1
  13.0 0.6 gather_fusion
  13.6 0.1 broadcast_bitcast_fusion.1
  13.7 0.3 copy.49
  14.0 0.0 copy-start.11
  14.0 0.1 multiply_reduce_fusion.7
  14.1 0.1 broadcast_multiply_fusion.3
  14.2 0.6 copy-done.11
  14.8 1.5 copy.58
  16.4 0.1 multiply_reduce_fusion.5
  16.5 0.1 and_reduce_fusion
  16.6 2.3 %copy.53 = f32[1,1,128,2048]{2,3,1,0:T(8,128)} copy(bf16[1,1,128,2048]{3,2,1,0:T(8,128)(2,1)} %param.7) | data formatting | bytes 1572864 | tf_op jit(solution)/shard_map/convert_element_type | solution.py:97
  18.9 0.6 gather_fusion.1
  19.5 1.1 broadcast_multiply_fusion.1
  20.6 12.6 %collective-permute-done = bf16[128,2048]{1,0:T(8,128)(2,1)} collective-permute-done((bf16[128,2048]{1,0:T(8,128)(2,1)}, bf16[128,2048]{1,0:T(8,128)(2,1)}, u32[]{:S(2)}, u32[]{:S(2)}) %collective-permute-start) | collective-permute-done | bytes 524320 | tf_op jit(solution)/shard_map/ppermute | solution.py:18
  33.2 1.2 copy.50
  34.4 0.1 multiply_reduce_fusion.6
  34.5 1.1 broadcast_multiply_fusion.2
  35.6 3.9 %fusion.49 = (f32[16,128]{1,0:T(8,128)S(1)}, f32[16,128,256]{2,1,0:T(8,128)}) fusion(pred[256]{0:T(512)(128)(4,1)S(1)} %broadcast_bitcast_fusion.1, f32[16,128]{1,0:T(8,128)S(1)} %bitcast.124, f32[128,16,128]{0,2,1:T(8,128)} %broadcast_multiply_fusion.2, f32[128,16,128]{0,2,1:T(8,128)S(1)} %broadcast_multiply_fusion.3, f32[16,128]{1,0:T(8,128)S(1)} %bitcast.119), kind=kOutput, calls=%fused_computation.119 | convolution fusion | flops 138412288 | bytes 4219136 | tf_op jit(solution)/shard_map/sub | solution.py:66
  39.5 2.8 %fusion.26 = f32[16,128,256]{2,1,0:T(8,128)S(1)} fusion(f32[128,16,128]{0,2,1:T(8,128)} %bitcast.110, f32[16,128]{1,0:T(8,128)S(1)} %bitcast.141, f32[16,128,256]{2,1,0:T(8,128)} %get-tuple-element.24, f32[16,128]{1,0:T(8,128)S(1)} %get-tuple-element.23), kind=kOutput, calls=%fused_computation.70 | convolution fusion | flops 135790592 | bytes 5259264 | tf_op jit(solution)/shard_map/hts,thd->shd/dot_general | solution.py:121
  42.4 0.0 copy-done
  42.4 0.0 copy-done.3
  42.4 0.3 copy-done.5
  42.7 2.2 multiply_reduce_fusion.1
  44.9 0.7 multiply_convert_fusion.3
  45.6 1.9 fusion.5
  47.6 0.0 copy-start.2
  47.6 1.9 multiply_reduce_fusion.3
  49.5 0.0 copy-done.2
  49.5 1.0 multiply_convert_fusion.7
  50.5 6.3 %collective-permute-start.2 = (bf16[128,16,128]{0,2,1:T(8,128)(2,1)}, bf16[128,16,128]{0,2,1:T(8,128)(2,1)}, u32[]{:S(2)}, u32[]{:S(2)}) collective-permute-start(bf16[128,16,128]{0,2,1:T(8,128)(2,1)} %multiply_convert_fusion.7), channel_id=1, source_target_pairs={{0,1},{1,0},{2,3},{3,2},{4,5},{5,4},{6,7},{7,6},{8,9},{9,8},{10,11... | collective-permute-start | bytes 1572872 | tf_op jit(solution)/shard_map/ppermute | solution.py:18
  56.8 0.1 broadcast_bitcast_fusion
  56.9 0.0 collective-permute-done.1
  56.9 1.2 copy.59
  58.1 0.1 multiply_reduce_fusion.4
  58.2 22.9 %collective-permute-done.2 = bf16[128,16,128]{0,2,1:T(8,128)(2,1)} collective-permute-done((bf16[128,16,128]{0,2,1:T(8,128)(2,1)}, bf16[128,16,128]{0,2,1:T(8,128)(2,1)}, u32[]{:S(2)}, u32[]{:S(2)}) %collective-permute-start.2) | collective-permute-done | bytes 524320 | tf_op jit(solution)/shard_map/ppermute | solution.py:18
  81.1 3.6 %convert_add_fusion = f32[128,16,128]{0,2,1:T(8,128)} fusion(bf16[128,16,128]{0,2,1:T(8,128)(2,1)} %collective-permute-done.2, f32[128,16,128]{0,2,1:T(8,128)} %bitcast.111, f32[128,16]{0,1:T(8,128)S(1)} %broadcast_multiply_fusion.7, f32[128,16]{0,1:T(8,128)S(1)} %add_rsqrt_fusion.3, f32[256,16,128]{0,2,1:T(8,128)} %copy-done.2, ...), kind=kLoop, calls=%fused_computation.45 | loop fusion | flops 2359296 | bytes 5791744 | tf_op jit(solution)/shard_map/add | solution.py:142
  84.7 2.6 %copy.62 = f32[128,2048]{1,0:T(8,128)} copy(f32[128,2048]{0,1:T(8,128)} %bitcast.114) | data formatting | bytes 2097152 | tf_op jit(solution)/shard_map/reshape | solution.py:146
  87.3 11.7 %collective-permute-start.3 = (f32[128,2048]{1,0:T(8,128)}, f32[128,2048]{1,0:T(8,128)}, u32[]{:S(2)}, u32[]{:S(2)}) collective-permute-start(f32[128,2048]{1,0:T(8,128)} %copy.62), channel_id=1, source_target_pairs={{16,0},{32,16},{48,32},{64,48},{80,64},{96,80},{112,96},{128,112},... | collective-permute-start | bytes 3145736 | tf_op jit(solution)/shard_map/ppermute | solution.py:24
  99.0 1.1 broadcast_multiply_fusion
  100.1 4.8 %fusion.50 = (f32[16,128]{1,0:T(8,128)S(1)}, f32[16,128,256]{2,1,0:T(8,128)}) fusion(pred[256]{0:T(512)(128)(4,1)S(1)} %broadcast_bitcast_fusion, f32[16,128]{1,0:T(8,128)S(1)} %bitcast.126, f32[128,16,128]{0,2,1:T(8,128)} %broadcast_multiply_fusion, f32[128,16,128]{0,2,1:T(8,128)} %broadcast_multiply_fusion.1, f32[16,128]{1,0:T(8,128)S(1)} %bitcast.121), kind=kOutput, calls=%fused_computation.120 | convolution fusion | flops 138412288 | bytes 4219136 | tf_op jit(solution)/shard_map/sub | solution.py:66
  104.9 2.6 %fusion.12 = f32[16,128]{1,0:T(8,128)S(1)} fusion(f32[128,16,128]{0,2,1:T(8,128)S(1)} %bitcast.113, f32[16,128]{1,0:T(8,128)S(1)} %bitcast.133, f32[128,16,128]{0,2,1:T(8,128)S(1)} %copy-done.1, f32[128,16,128]{0,2,1:T(8,128)S(1)} %broadcast_multiply_fusion.3, f32[16,128,256]{2,1,0:T(8,128)} %get-tuple-element.24, f32[16,128]{1,0:T(8,128)S(1)} %get-tuple-element.23), kind=kOutput, calls=%fused_computation.37 | convolution fusion | flops 137361408 | bytes 5267456 | tf_op jit(solution)/shard_map/hts,shd->thd/dot_general | solution.py:69
  107.5 14.2 %collective-permute-done.3 = f32[128,2048]{1,0:T(8,128)} collective-permute-done((f32[128,2048]{1,0:T(8,128)}, f32[128,2048]{1,0:T(8,128)}, u32[]{:S(2)}, u32[]{:S(2)}) %collective-permute-start.3) | collective-permute-done | bytes 1048608 | tf_op jit(solution)/shard_map/ppermute | solution.py:24
  121.7 1.3 convert_select_fusion
  123.1 1.3 copy.63
  124.4 3.4 %multiply_reduce_fusion = (f32[16,128]{1,0:T(8,128)S(1)}, f32[16,128,256]{2,1,0:T(8,128)S(1)}) fusion(f32[16,128,256]{2,1,0:T(8,128)S(1)} %copy-done.6, f32[16,128]{1,0:T(8,128)S(1)} %get-tuple-element.28, f32[16,128]{1,0:T(8,128)S(1)} %bitcast.134, f32[128,16,128]{0,2,1:T(8,128)} %broadcast_multiply_fusion, f32[128,16,128]{0,2,1:T(8,128)} %broadcast_multiply_fusion.1, ...), kind=kOutput, calls=%fused_computation.17 | convolution fusion | flops 137885696 | bytes 7372800 | tf_op jit(solution)/shard_map/thd,shd->hts/dot_general | solution.py:71
  127.8 0.8 multiply_convert_fusion
  128.6 0.4 copy-done.7
  129.0 0.3 copy-done.8
  129.4 0.7 fusion.13
  130.0 0.7 fusion.3
  130.7 0.5 copy-done.9
  131.3 1.1 fusion.2
  132.4 1.2 fusion.14
  133.6 0.1 fusion.32
  133.7 86.5 %psum.7 = f32[1,4,2048]{2,1,0:T(4,128)} all-reduce(f32[1,4,2048]{2,1,0:T(4,128)S(1)} %fusion.32), channel_id=1, replica_groups=mesh['segment'=32,'dp'=8,'seq'=2] {'dp','seq'}, use_global_device_ids=true, to_apply=%region_22.23 | all-reduce | flops 8192 | bytes 65536 | tf_op jit(solution)/shard_map/psum | solution.py:152
  (28 shorter events, 0.1 us)
Async XLA Ops:
  0.0 12.8 %copy-start.13 = (s32[1,2,1,2]{3,2,1,0:T(1,128)S(1)}, s32[1,2,1,2]{3,2,1,0:T(1,128)}, u32[]{:S(2)}) copy-start(s32[1,2,1,2]{3,2,1,0:T(1,128)} %param.11) | copy-start | bytes 52
  0.0 12.8 %copy-start.12 = (s32[1,2,1,2,2]{4,3,2,1,0:T(2,128)S(1)}, s32[1,2,1,2,2]{4,3,2,1,0:T(2,128)}, u32[]{:S(2)}) copy-start(s32[1,2,1,2,2]{4,3,2,1,0:T(2,128)} %param.10) | copy-start | bytes 100
  2.7 30.5 %collective-permute-start = (bf16[128,2048]{1,0:T(8,128)(2,1)}, bf16[128,2048]{1,0:T(8,128)(2,1)}, u32[]{:S(2)}, u32[]{:S(2)}) collective-permute-start(bf16[128,2048]{1,0:T(8,128)(2,1)} %get-tuple-element.12), channel_id=1, source_target_pairs={{0,1},{1,0},{2,3},{3,2},{4,5},{5,4},{6,7},{7,6},{8,9},{9,8},{10,11... | collective-permute-start | bytes 1572872 | tf_op jit(solution)/shard_map/ppermute | solution.py:18
  7.8 49.1 %collective-permute-start.1 = (bf16[128,2048]{1,0:T(8,128)(2,1)}, bf16[128,2048]{1,0:T(8,128)(2,1)}, u32[]{:S(2)}, u32[]{:S(2)}) collective-permute-start(bf16[128,2048]{1,0:T(8,128)(2,1)} %get-tuple-element.13), channel_id=1, source_target_pairs={{0,1},{1,0},{2,3},{3,2},{4,5},{5,4},{6,7},{7,6},{8,9},{9,8},{10,11... | collective-permute-start | bytes 1572872 | tf_op jit(solution)/shard_map/ppermute | solution.py:18
  14.0 0.8 copy-start.11
  39.5 2.9 %copy-start = (f32[128,16,128]{0,2,1:T(8,128)S(1)}, f32[128,16,128]{0,2,1:T(8,128)}, u32[]{:S(2)}) copy-start(f32[128,16,128]{0,2,1:T(8,128)} %broadcast_multiply_fusion.2) | copy-start | bytes 3145732
  39.5 2.9 %copy-start.3 = (f32[1,1,128,2048]{2,3,1,0:T(8,128)S(1)}, f32[1,1,128,2048]{2,3,1,0:T(8,128)}, u32[]{:S(2)}) copy-start(f32[1,1,128,2048]{2,3,1,0:T(8,128)} %copy.53) | copy-start | bytes 3145732
  39.5 3.2 %copy-start.5 = (f32[16,128,256]{2,1,0:T(8,128)S(1)}, f32[16,128,256]{2,1,0:T(8,128)}, u32[]{:S(2)}) copy-start(f32[16,128,256]{2,1,0:T(8,128)} %get-tuple-element.24) | copy-start | bytes 6291460
  47.6 1.9 copy-start.2
  50.5 30.6 %collective-permute-start.2 = (bf16[128,16,128]{0,2,1:T(8,128)(2,1)}, bf16[128,16,128]{0,2,1:T(8,128)(2,1)}, u32[]{:S(2)}, u32[]{:S(2)}) collective-permute-start(bf16[128,16,128]{0,2,1:T(8,128)(2,1)} %multiply_convert_fusion.7), channel_id=1, source_target_pairs={{0,1},{1,0},{2,3},{3,2},{4,5},{5,4},{6,7},{7,6},{8,9},{9,8},{10,11... | collective-permute-start | bytes 1572872 | tf_op jit(solution)/shard_map/ppermute | solution.py:18
  87.3 34.4 %collective-permute-start.3 = (f32[128,2048]{1,0:T(8,128)}, f32[128,2048]{1,0:T(8,128)}, u32[]{:S(2)}, u32[]{:S(2)}) collective-permute-start(f32[128,2048]{1,0:T(8,128)} %copy.62), channel_id=1, source_target_pairs={{16,0},{32,16},{48,32},{64,48},{80,64},{96,80},{112,96},{128,112},... | collective-permute-start | bytes 3145736 | tf_op jit(solution)/shard_map/ppermute | solution.py:24
  100.1 4.8 %copy-start.1 = (f32[128,16,128]{0,2,1:T(8,128)S(1)}, f32[128,16,128]{0,2,1:T(8,128)}, u32[]{:S(2)}) copy-start(f32[128,16,128]{0,2,1:T(8,128)} %broadcast_multiply_fusion.2) | copy-start | bytes 3145732
  100.1 4.8 %copy-start.4 = (f32[1,1,128,2048]{2,3,1,0:T(8,128)S(1)}, f32[1,1,128,2048]{2,3,1,0:T(8,128)}, u32[]{:S(2)}) copy-start(f32[1,1,128,2048]{2,3,1,0:T(8,128)} %copy.53) | copy-start | bytes 3145732
  104.9 16.8 %copy-start.10 = (bf16[1,1,128,2048]{3,2,1,0:T(8,128)(2,1)S(1)}, bf16[1,1,128,2048]{3,2,1,0:T(8,128)(2,1)}, u32[]{:S(2)}) copy-start(bf16[1,1,128,2048]{3,2,1,0:T(8,128)(2,1)} %param.8) | copy-start | bytes 1572868
  107.5 16.9 %copy-start.6 = (f32[16,128,256]{2,1,0:T(8,128)S(1)}, f32[16,128,256]{2,1,0:T(8,128)}, u32[]{:S(2)}) copy-start(f32[16,128,256]{2,1,0:T(8,128)} %get-tuple-element.29) | copy-start | bytes 6291460
  127.8 1.2 copy-start.7
  127.8 1.5 copy-start.8
  130.0 1.2 copy-start.9
where the time goes:
time: 221 us; the launch traced here: 220 us
  blocking collectives  86.5 us (39%)
  waiting for transfers between devices  49.7 us (22%)
  starting transfers between devices  27.7 us (13%)
  matrix products  27.2 us (12%)
  other arithmetic  14.5 us (7%)
  local copies, waits for them, and re-layouts  14.3 us (6%)
    psum x1, blocking collectives, shards(): summed = lax.psum(totals.reshape(4, channels), ('dp', 'seq'))  86.5 us
    ppermute x3, waiting for transfers between devices, partner(): return lax.ppermute(block, axis, route)  35.5 us
    ppermute x3, starting transfers between devices, partner(): return lax.ppermute(block, axis, route)  16 us
    ppermute x1, waiting for transfers between devices, from_behind(): return lax.ppermute(block, axis, route)  14.2 us
    ppermute x1, starting transfers between devices, from_behind(): return lax.ppermute(block, axis, route)  11.7 us
    sub x2, matrix products, attend(): exped = jnp.exp(scores - jnp.max(scores, axis=-1, keepdims=True))  8.66 us
    dot_general x2, matrix products, attend(): jnp.einsum('thd,shd->hts', grad_out, val_mat, preferred_element_type=jnp....  5.55 us
  transfers between devices with their start and end apart: 4, of which 3 were waited for; matrix products, arithmetic and copies ran while one was open for 16% of the time, Pallas kernels for 0%

commit v1 on v0

--- a/solution.py
+++ b/solution.py
@@ -149,7 +149,8 @@
                 uppermost_result_derivative[step_index, 0].astype(jnp.float32),
                 received,
             )
-    summed = lax.psum(totals.reshape(4, channels), ("dp", "seq"))
+    partial = lax.psum(totals.reshape(4, channels), "seq")
+    summed = lax.psum(partial, "dp")
     return summed[None]
 
 

time: 221 us -> 172 us (0.78)
  the two profiles are of different devices: /device:TPU:24 before, /device:TPU:56 now
where the time goes in v1:
time: 172 us; the launch traced here: 171 us
  waiting for transfers between devices  51 us (30%)
  blocking collectives  39.3 us (23%)
  matrix products  27.2 us (16%)
  starting transfers between devices  24.9 us (14%)
  other arithmetic  14.5 us (8%)
  local copies, waits for them, and re-layouts  14.3 us (8%)
    ppermute x3, waiting for transfers between devices, partner(): return lax.ppermute(block, axis, route)  37.9 us
    psum x1, blocking collectives, shards(): summed = lax.psum(partial, 'dp')  24.2 us
    psum x1, blocking collectives, shards(): partial = lax.psum(totals.reshape(4, channels), 'seq')  15.1 us
    ppermute x3, starting transfers between devices, partner(): return lax.ppermute(block, axis, route)  13.2 us
    ppermute x1, waiting for transfers between devices, from_behind(): return lax.ppermute(block, axis, route)  13.1 us
    ppermute x1, starting transfers between devices, from_behind(): return lax.ppermute(block, axis, route)  11.7 us
    sub x2, matrix products, attend(): exped = jnp.exp(scores - jnp.max(scores, axis=-1, keepdims=True))  8.66 us
    dot_general x2, matrix products, attend(): jnp.einsum('thd,shd->hts', grad_out, val_mat, preferred_element_type=jnp....  5.55 us
  transfers between devices with their start and end apart: 4, of which 3 were waited for; matrix products, arithmetic and copies ran while one was open for 20% of the time, Pallas kernels for 0%

profile of v1, /device:TPU:56, one launch (start us, length us, event | category | flops | bytes accessed | tf_op | source)
XLA Modules:
  0.0 171.4 jit_solution(16362318808093734765)
XLA Ops:
  0.0 2.7 %slice_convert_fusion = (f32[1,1,1,128,2048]{4,3,2,1,0:T(8,128)}, bf16[128,2048]{1,0:T(8,128)(2,1)}, bf16[128,2048]{1,0:T(8,128)(2,1)}, f32[1,1,1,128,2048]{4,3,2,1,0:T(8,128)S(1)}) fusion(bf16[1,2,1,128,2048]{4,3,2,1,0:T(8,128)(2,1)} %param.6), kind=kLoop, calls=%fused_computation.75 | loop fusion | flops 524288 | bytes 4194304 | tf_op jit(solution)/shard_map/convert_element_type | solution.py:28
  2.7 4.7 %collective-permute-start = (bf16[128,2048]{1,0:T(8,128)(2,1)}, bf16[128,2048]{1,0:T(8,128)(2,1)}, u32[]{:S(2)}, u32[]{:S(2)}) collective-permute-start(bf16[128,2048]{1,0:T(8,128)(2,1)} %get-tuple-element.12), channel_id=1, source_target_pairs={{0,1},{1,0},{2,3},{3,2},{4,5},{5,4},{6,7},{7,6},{8,9},{9,8},{10,11... | collective-permute-start | bytes 1572872 | tf_op jit(solution)/shard_map/ppermute | solution.py:18
  7.4 5.0 %collective-permute-start.1 = (bf16[128,2048]{1,0:T(8,128)(2,1)}, bf16[128,2048]{1,0:T(8,128)(2,1)}, u32[]{:S(2)}, u32[]{:S(2)}) collective-permute-start(bf16[128,2048]{1,0:T(8,128)(2,1)} %get-tuple-element.13), channel_id=1, source_target_pairs={{0,1},{1,0},{2,3},{3,2},{4,5},{5,4},{6,7},{7,6},{8,9},{9,8},{10,11... | collective-permute-start | bytes 1572872 | tf_op jit(solution)/shard_map/ppermute | solution.py:18
  12.5 0.1 pad_bitcast_fusion
  12.6 0.2 or_reduce_fusion
  12.8 0.0 copy-done.13
  12.8 0.0 copy-done.12
  12.8 0.1 iota_compare_fusion
  12.9 0.1 and_reduce_fusion.1
  13.0 0.6 gather_fusion
  13.6 0.1 broadcast_bitcast_fusion.1
  13.7 0.3 copy.49
  14.0 0.0 copy-start.11
  14.0 0.1 multiply_reduce_fusion.7
  14.1 0.1 broadcast_multiply_fusion.3
  14.2 0.6 copy-done.11
  14.8 1.5 copy.58
  16.4 0.1 multiply_reduce_fusion.5
  16.5 0.1 and_reduce_fusion
  16.6 2.3 %copy.53 = f32[1,1,128,2048]{2,3,1,0:T(8,128)} copy(bf16[1,1,128,2048]{3,2,1,0:T(8,128)(2,1)} %param.7) | data formatting | bytes 1572864 | tf_op jit(solution)/shard_map/convert_element_type | solution.py:97
  18.9 0.6 gather_fusion.1
  19.5 1.1 broadcast_multiply_fusion.1
  20.6 13.8 %collective-permute-done = bf16[128,2048]{1,0:T(8,128)(2,1)} collective-permute-done((bf16[128,2048]{1,0:T(8,128)(2,1)}, bf16[128,2048]{1,0:T(8,128)(2,1)}, u32[]{:S(2)}, u32[]{:S(2)}) %collective-permute-start) | collective-permute-done | bytes 524320 | tf_op jit(solution)/shard_map/ppermute | solution.py:18
  34.4 1.2 copy.50
  35.7 0.1 multiply_reduce_fusion.6
  35.8 1.1 broadcast_multiply_fusion.2
  36.9 3.9 %fusion.48 = (f32[16,128]{1,0:T(8,128)S(1)}, f32[16,128,256]{2,1,0:T(8,128)}) fusion(pred[256]{0:T(512)(128)(4,1)S(1)} %broadcast_bitcast_fusion.1, f32[16,128]{1,0:T(8,128)S(1)} %bitcast.124, f32[128,16,128]{0,2,1:T(8,128)} %broadcast_multiply_fusion.2, f32[128,16,128]{0,2,1:T(8,128)S(1)} %broadcast_multiply_fusion.3, f32[16,128]{1,0:T(8,128)S(1)} %bitcast.119), kind=kOutput, calls=%fused_computation.118 | convolution fusion | flops 138412288 | bytes 4219136 | tf_op jit(solution)/shard_map/sub | solution.py:66
  40.8 2.8 %fusion.26 = f32[16,128,256]{2,1,0:T(8,128)S(1)} fusion(f32[128,16,128]{0,2,1:T(8,128)} %bitcast.109, f32[16,128]{1,0:T(8,128)S(1)} %bitcast.141, f32[16,128,256]{2,1,0:T(8,128)} %get-tuple-element.24, f32[16,128]{1,0:T(8,128)S(1)} %get-tuple-element.23), kind=kOutput, calls=%fused_computation.70 | convolution fusion | flops 135790592 | bytes 5259264 | tf_op jit(solution)/shard_map/hts,thd->shd/dot_general | solution.py:121
  43.6 0.0 copy-done
  43.6 0.0 copy-done.3
  43.6 0.3 copy-done.5
  43.9 2.2 %multiply_reduce_fusion.1 = (f32[16,128]{1,0:T(8,128)S(1)}, f32[16,128,256]{2,1,0:T(8,128)S(1)}) fusion(f32[16,128,256]{2,1,0:T(8,128)S(1)} %copy-done.5, f32[16,128]{1,0:T(8,128)S(1)} %get-tuple-element.23, f32[16,128]{1,0:T(8,128)S(1)} %bitcast.131, f32[128,16,128]{0,2,1:T(8,128)S(1)} %copy-done, f32[128,16,128]{0,2,1:T(8,128)S(1)} %broadcast_multiply_fusion.3, ...), kind=kOutput, calls=%fused_computation.23 | convolution fusion | flops 137885696 | bytes 7372800 | tf_op jit(solution)/shard_map/thd,shd->hts/dot_general | solution.py:71
  46.1 0.7 multiply_convert_fusion.3
  46.9 1.9 %fusion.5 = (f32[16,128]{1,0:T(8,128)S(1)}, f32[16,128]{1,0:T(8,128)S(1)}, f32[256,16,128]{0,2,1:T(8,128)S(1)}) fusion(f32[128,16,128]{0,2,1:T(8,128)S(1)} %copy-done, f32[128,16,128]{0,2,1:T(8,128)S(1)} %broadcast_multiply_fusion.3, f32[16,128,256]{2,1,0:T(8,128)S(1)} %fusion.26, f32[16,128]{1,0:T(8,128)S(1)} %bitcast.132, ...), kind=kOutput, calls=%fused_computation.15 | convolution fusion | flops 139456512 | bytes 7380992 | tf_op jit(solution)/shard_map/hts,thd->shd/dot_general | solution.py:118
  48.8 0.0 copy-start.2
  48.8 1.9 %multiply_reduce_fusion.3 = (f32[128,16]{0,1:T(8,128)S(1)}, f32[128,16]{0,1:T(8,128)S(1)}, f32[16,128]{1,0:T(8,128)S(1)}, f32[16,128,128]{2,1,0:T(8,128)}) fusion(f32[128,16,128]{0,2,1:T(8,128)S(1)} %broadcast_multiply_fusion.3, f32[256,16,128]{0,2,1:T(8,128)S(1)} %get-tuple-element.10, f32[16,128]{1,0:T(8,128)S(1)} %broadcast_multiply_fusion.5, ...), kind=kOutput, calls=%fused_computation.48 | convolution fusion | flops 138143744 | bytes 8429568 | tf_op jit(solution)/shard_map/hts,shd->thd/dot_general | solution.py:114
  50.8 1.0 multiply_convert_fusion.7
  51.8 3.5 %collective-permute-start.2 = (bf16[128,16,128]{0,2,1:T(8,128)(2,1)}, bf16[128,16,128]{0,2,1:T(8,128)(2,1)}, u32[]{:S(2)}, u32[]{:S(2)}) collective-permute-start(bf16[128,16,128]{0,2,1:T(8,128)(2,1)} %multiply_convert_fusion.7), channel_id=1, source_target_pairs={{0,1},{1,0},{2,3},{3,2},{4,5},{5,4},{6,7},{7,6},{8,9},{9,8},{10,11... | collective-permute-start | bytes 1572872 | tf_op jit(solution)/shard_map/ppermute | solution.py:18
  55.2 0.1 broadcast_bitcast_fusion
  55.3 0.0 collective-permute-done.1
  55.3 1.2 copy.59
  56.6 0.1 multiply_reduce_fusion.4
  56.7 24.1 %collective-permute-done.2 = bf16[128,16,128]{0,2,1:T(8,128)(2,1)} collective-permute-done((bf16[128,16,128]{0,2,1:T(8,128)(2,1)}, bf16[128,16,128]{0,2,1:T(8,128)(2,1)}, u32[]{:S(2)}, u32[]{:S(2)}) %collective-permute-start.2) | collective-permute-done | bytes 524320 | tf_op jit(solution)/shard_map/ppermute | solution.py:18
  80.7 3.6 %convert_add_fusion = f32[128,16,128]{0,2,1:T(8,128)} fusion(bf16[128,16,128]{0,2,1:T(8,128)(2,1)} %collective-permute-done.2, f32[128,16,128]{0,2,1:T(8,128)} %bitcast.110, f32[128,16]{0,1:T(8,128)S(1)} %broadcast_multiply_fusion.7, f32[128,16]{0,1:T(8,128)S(1)} %add_rsqrt_fusion.3, f32[256,16,128]{0,2,1:T(8,128)} %copy-done.2, ...), kind=kLoop, calls=%fused_computation.45 | loop fusion | flops 2359296 | bytes 5791744 | tf_op jit(solution)/shard_map/add | solution.py:142
  84.3 2.6 %copy.62 = f32[128,2048]{1,0:T(8,128)} copy(f32[128,2048]{0,1:T(8,128)} %bitcast.113) | data formatting | bytes 2097152 | tf_op jit(solution)/shard_map/reshape | solution.py:146
  86.9 11.7 %collective-permute-start.3 = (f32[128,2048]{1,0:T(8,128)}, f32[128,2048]{1,0:T(8,128)}, u32[]{:S(2)}, u32[]{:S(2)}) collective-permute-start(f32[128,2048]{1,0:T(8,128)} %copy.62), channel_id=1, source_target_pairs={{16,0},{32,16},{48,32},{64,48},{80,64},{96,80},{112,96},{128,112},... | collective-permute-start | bytes 3145736 | tf_op jit(solution)/shard_map/ppermute | solution.py:24
  98.6 1.1 broadcast_multiply_fusion
  99.7 4.8 %fusion.49 = (f32[16,128]{1,0:T(8,128)S(1)}, f32[16,128,256]{2,1,0:T(8,128)}) fusion(pred[256]{0:T(512)(128)(4,1)S(1)} %broadcast_bitcast_fusion, f32[16,128]{1,0:T(8,128)S(1)} %bitcast.126, f32[128,16,128]{0,2,1:T(8,128)} %broadcast_multiply_fusion, f32[128,16,128]{0,2,1:T(8,128)} %broadcast_multiply_fusion.1, f32[16,128]{1,0:T(8,128)S(1)} %bitcast.121), kind=kOutput, calls=%fused_computation.119 | convolution fusion | flops 138412288 | bytes 4219136 | tf_op jit(solution)/shard_map/sub | solution.py:66
  104.5 2.6 %fusion.12 = f32[16,128]{1,0:T(8,128)S(1)} fusion(f32[128,16,128]{0,2,1:T(8,128)S(1)} %bitcast.112, f32[16,128]{1,0:T(8,128)S(1)} %bitcast.133, f32[128,16,128]{0,2,1:T(8,128)S(1)} %copy-done.1, f32[128,16,128]{0,2,1:T(8,128)S(1)} %broadcast_multiply_fusion.3, f32[16,128,256]{2,1,0:T(8,128)} %get-tuple-element.24, f32[16,128]{1,0:T(8,128)S(1)} %get-tuple-element.23), kind=kOutput, calls=%fused_computation.37 | convolution fusion | flops 137361408 | bytes 5267456 | tf_op jit(solution)/shard_map/hts,shd->thd/dot_general | solution.py:69
  107.1 13.1 %collective-permute-done.3 = f32[128,2048]{1,0:T(8,128)} collective-permute-done((f32[128,2048]{1,0:T(8,128)}, f32[128,2048]{1,0:T(8,128)}, u32[]{:S(2)}, u32[]{:S(2)}) %collective-permute-start.3) | collective-permute-done | bytes 1048608 | tf_op jit(solution)/shard_map/ppermute | solution.py:24
  120.2 1.3 convert_select_fusion
  121.5 1.3 copy.63
  122.9 3.4 %multiply_reduce_fusion = (f32[16,128]{1,0:T(8,128)S(1)}, f32[16,128,256]{2,1,0:T(8,128)S(1)}) fusion(f32[16,128,256]{2,1,0:T(8,128)S(1)} %copy-done.6, f32[16,128]{1,0:T(8,128)S(1)} %get-tuple-element.28, f32[16,128]{1,0:T(8,128)S(1)} %bitcast.134, f32[128,16,128]{0,2,1:T(8,128)} %broadcast_multiply_fusion, f32[128,16,128]{0,2,1:T(8,128)} %broadcast_multiply_fusion.1, ...), kind=kOutput, calls=%fused_computation.17 | convolution fusion | flops 137885696 | bytes 7372800 | tf_op jit(solution)/shard_map/thd,shd->hts/dot_general | solution.py:71
  126.2 0.8 multiply_convert_fusion
  127.0 0.4 copy-done.7
  127.5 0.3 copy-done.8
  127.8 0.7 fusion.13
  128.5 0.7 fusion.3
  129.2 0.5 copy-done.9
  129.7 1.1 fusion.2
  130.8 1.2 fusion.14
  132.0 0.1 maximum_add_fusion
  132.1 15.1 %psum.14 = f32[4,2048]{1,0:T(4,128)S(1)} all-reduce(f32[4,2048]{1,0:T(4,128)S(1)} %maximum_add_fusion), channel_id=1, replica_groups=mesh['segment'=32,'dp'=8,'seq'=2] {'seq'}, use_global_device_ids=true, to_apply=%region_22.23 | all-reduce | flops 8192 | bytes 65536 | tf_op jit(solution)/shard_map/psum | solution.py:152
  147.2 24.2 %psum.15 = f32[1,4,2048]{2,1,0:T(4,128)} all-reduce(f32[1,4,2048]{2,1,0:T(4,128)S(1)} %bitcast.117), channel_id=1, replica_groups=mesh['segment'=32,'dp'=8,'seq'=2] {'dp'}, use_global_device_ids=true, to_apply=%region_23.24 | all-reduce | flops 8192 | bytes 65536 | tf_op jit(solution)/shard_map/psum | solution.py:153
  (29 shorter events, 0.1 us)
Async XLA Ops:
  0.0 12.8 %copy-start.13 = (s32[1,2,1,2]{3,2,1,0:T(1,128)S(1)}, s32[1,2,1,2]{3,2,1,0:T(1,128)}, u32[]{:S(2)}) copy-start(s32[1,2,1,2]{3,2,1,0:T(1,128)} %param.11) | copy-start | bytes 52
  0.0 12.8 %copy-start.12 = (s32[1,2,1,2,2]{4,3,2,1,0:T(2,128)S(1)}, s32[1,2,1,2,2]{4,3,2,1,0:T(2,128)}, u32[]{:S(2)}) copy-start(s32[1,2,1,2,2]{4,3,2,1,0:T(2,128)} %param.10) | copy-start | bytes 100
  2.7 31.7 %collective-permute-start = (bf16[128,2048]{1,0:T(8,128)(2,1)}, bf16[128,2048]{1,0:T(8,128)(2,1)}, u32[]{:S(2)}, u32[]{:S(2)}) collective-permute-start(bf16[128,2048]{1,0:T(8,128)(2,1)} %get-tuple-element.12), channel_id=1, source_target_pairs={{0,1},{1,0},{2,3},{3,2},{4,5},{5,4},{6,7},{7,6},{8,9},{9,8},{10,11... | collective-permute-start | bytes 1572872 | tf_op jit(solution)/shard_map/ppermute | solution.py:18
  7.4 47.9 %collective-permute-start.1 = (bf16[128,2048]{1,0:T(8,128)(2,1)}, bf16[128,2048]{1,0:T(8,128)(2,1)}, u32[]{:S(2)}, u32[]{:S(2)}) collective-permute-start(bf16[128,2048]{1,0:T(8,128)(2,1)} %get-tuple-element.13), channel_id=1, source_target_pairs={{0,1},{1,0},{2,3},{3,2},{4,5},{5,4},{6,7},{7,6},{8,9},{9,8},{10,11... | collective-permute-start | bytes 1572872 | tf_op jit(solution)/shard_map/ppermute | solution.py:18
  14.0 0.8 copy-start.11
  40.8 2.9 %copy-start = (f32[128,16,128]{0,2,1:T(8,128)S(1)}, f32[128,16,128]{0,2,1:T(8,128)}, u32[]{:S(2)}) copy-start(f32[128,16,128]{0,2,1:T(8,128)} %broadcast_multiply_fusion.2) | copy-start | bytes 3145732
  40.8 2.9 %copy-start.3 = (f32[1,1,128,2048]{2,3,1,0:T(8,128)S(1)}, f32[1,1,128,2048]{2,3,1,0:T(8,128)}, u32[]{:S(2)}) copy-start(f32[1,1,128,2048]{2,3,1,0:T(8,128)} %copy.53) | copy-start | bytes 3145732
  40.8 3.2 %copy-start.5 = (f32[16,128,256]{2,1,0:T(8,128)S(1)}, f32[16,128,256]{2,1,0:T(8,128)}, u32[]{:S(2)}) copy-start(f32[16,128,256]{2,1,0:T(8,128)} %get-tuple-element.24) | copy-start | bytes 6291460
  48.8 1.9 %copy-start.2 = (f32[256,16,128]{0,2,1:T(8,128)}, f32[256,16,128]{0,2,1:T(8,128)S(1)}, u32[]{:S(2)}) copy-start(f32[256,16,128]{0,2,1:T(8,128)S(1)} %get-tuple-element.10) | copy-start | bytes 6291460
  51.8 29.0 %collective-permute-start.2 = (bf16[128,16,128]{0,2,1:T(8,128)(2,1)}, bf16[128,16,128]{0,2,1:T(8,128)(2,1)}, u32[]{:S(2)}, u32[]{:S(2)}) collective-permute-start(bf16[128,16,128]{0,2,1:T(8,128)(2,1)} %multiply_convert_fusion.7), channel_id=1, source_target_pairs={{0,1},{1,0},{2,3},{3,2},{4,5},{5,4},{6,7},{7,6},{8,9},{9,8},{10,11... | collective-permute-start | bytes 1572872 | tf_op jit(solution)/shard_map/ppermute | solution.py:18
  86.9 33.2 %collective-permute-start.3 = (f32[128,2048]{1,0:T(8,128)}, f32[128,2048]{1,0:T(8,128)}, u32[]{:S(2)}, u32[]{:S(2)}) collective-permute-start(f32[128,2048]{1,0:T(8,128)} %copy.62), channel_id=1, source_target_pairs={{16,0},{32,16},{48,32},{64,48},{80,64},{96,80},{112,96},{128,112},... | collective-permute-start | bytes 3145736 | tf_op jit(solution)/shard_map/ppermute | solution.py:24
  99.7 4.8 %copy-start.1 = (f32[128,16,128]{0,2,1:T(8,128)S(1)}, f32[128,16,128]{0,2,1:T(8,128)}, u32[]{:S(2)}) copy-start(f32[128,16,128]{0,2,1:T(8,128)} %broadcast_multiply_fusion.2) | copy-start | bytes 3145732
  99.7 4.8 %copy-start.4 = (f32[1,1,128,2048]{2,3,1,0:T(8,128)S(1)}, f32[1,1,128,2048]{2,3,1,0:T(8,128)}, u32[]{:S(2)}) copy-start(f32[1,1,128,2048]{2,3,1,0:T(8,128)} %copy.53) | copy-start | bytes 3145732
  104.5 15.7 %copy-start.10 = (bf16[1,1,128,2048]{3,2,1,0:T(8,128)(2,1)S(1)}, bf16[1,1,128,2048]{3,2,1,0:T(8,128)(2,1)}, u32[]{:S(2)}) copy-start(bf16[1,1,128,2048]{3,2,1,0:T(8,128)(2,1)} %param.8) | copy-start | bytes 1572868
  107.1 15.8 %copy-start.6 = (f32[16,128,256]{2,1,0:T(8,128)S(1)}, f32[16,128,256]{2,1,0:T(8,128)}, u32[]{:S(2)}) copy-start(f32[16,128,256]{2,1,0:T(8,128)} %get-tuple-element.29) | copy-start | bytes 6291460
  126.2 1.2 copy-start.7
  126.2 1.5 copy-start.8
  128.5 1.2 copy-start.9
